TPU v7x, 768 devices: a whole 4x8x12 slice. The times are simulated.
768 devices in a mesh: batch: 8 (over y), dir: 96 (over z, x, core).
Axes of the slice: x: 4, y: 8, z: 12, core: 2. Of those that a mesh axis runs over, the one named last changes fastest.
Arguments:
- embeddings: bfloat16 [3072, 2048], P(('batch', 'dir')), may hold values from -13 to 13
- directions: bfloat16 [2048, 24576], P(None, 'dir'), may hold values from -0.125 to 0.125
Outputs:
- grad_embed: float32 [3072, 2048], P(('batch', 'dir'))
All inputs are finite; a program needn't handle non-finite values.
Results may differ from a plain program's by a relative error of at most 0.0016.
Values may be sent and summed in bfloat16 or wider, within the bound.
No kernel may reach another device: no remote copies, remote signals or barrier semaphores. Data moves between devices by JAX's collectives and lax.ppermute only.
A program may use at most 32 MiB of HBM per device.

v0:
```python
import functools
import math

import jax
import jax.numpy as jnp
from jax import lax
from jax.experimental import pallas as pl
from jax.experimental.pallas import tpu as pltpu
from jax.sharding import Mesh, PartitionSpec as P


KNOTS = 17
STEP = 3.0 / (KNOTS - 1)
KNOT = [k * STEP for k in range(KNOTS)]
TARGET = [math.exp(-0.5 * t * t) for t in KNOT]
WEIGHT = [(0.5 if k in (0, KNOTS - 1) else 1.0) * STEP * TARGET[k] for k in range(KNOTS)]
TURN = (6.28125, 0.0019340515136719, 1.2556659146e-06)
TILE = 16
F32 = jnp.float32
BF16 = jnp.bfloat16
LINK = jnp.float16


def base_angle(proj):
    theta = proj * STEP
    turns = jnp.round(theta * (0.5 / math.pi))
    q = 0.25 * (((theta - turns * TURN[0]) - turns * TURN[1]) - turns * TURN[2])
    z = q * q
    s = q * (1.0 + z * (-1.0 / 6 + z * (1.0 / 120 + z * (-1.0 / 5040 + z * (1.0 / 362880)))))
    c = 1.0 - z * (0.5 + z * (-1.0 / 24 + z * (1.0 / 720 + z * (-1.0 / 40320))))
    s2 = 2.0 * s * c
    c2 = 1.0 - 2.0 * s * s
    return 1.0 - 2.0 * s2 * s2, 2.0 * s2 * c2


def unit_kernel(dir_ref, unit_ref):
    width = dir_ref.shape[1]
    rows = 256
    total = jnp.zeros((8, width), F32)
    for i in range(dir_ref.shape[0] // rows):
        w = dir_ref[pl.ds(i * rows, rows), :].astype(F32)
        total = total + jnp.sum((w * w).reshape(rows // 8, 8, width), axis=0)
    inv = 1.0 / jnp.sqrt(jnp.sum(total, axis=0, keepdims=True) + 1e-06)
    for i in range(dir_ref.shape[0] // rows):
        w = dir_ref[pl.ds(i * rows, rows), :].astype(F32)
        unit_ref[pl.ds(i * rows, rows), :] = (w * inv).astype(BF16)


def sums_kernel(rows_ref, unit_ref, more_ref, c_ref, s_ref, out_ref, proj_ref, acc_ref):
    rows, width = proj_ref.shape
    half = width // 2
    proj_ref[:, pl.ds(0, half)] = jnp.dot(rows_ref[...], unit_ref[...], preferred_element_type=F32)
    proj_ref[:, pl.ds(half, half)] = jnp.dot(rows_ref[...], more_ref[...], preferred_element_type=F32)
    acc_ref[...] = jnp.zeros_like(acc_ref)

    def fold(v):
        return jnp.sum(v.reshape(TILE // 8, 8, width), axis=0)

    @pl.loop(0, rows // TILE)
    def _(i):
        at = pl.ds(pl.multiple_of(i * TILE, TILE), TILE)
        c1, s1 = base_angle(proj_ref[at, :])
        c_ref[at, :] = c1
        s_ref[at, :] = s1
        two = c1 + c1
        acc_ref[0] += fold(c1)
        acc_ref[KNOTS - 1] += fold(s1)
        cp, sp, cc, sc = jnp.ones_like(c1), jnp.zeros_like(c1), c1, s1
        for k in range(1, KNOTS - 1):
            cp, cc = cc, two * cc - cp
            sp, sc = sc, two * sc - sp
            acc_ref[k] += fold(cc)
            acc_ref[KNOTS - 1 + k] += fold(sc)

    out_ref[...] = jnp.sum(acc_ref[...], axis=1)
    for k in range(1, KNOTS):
        out_ref[pl.ds(k - 1, 1), :] -= rows * TARGET[k]


def grad_kernel(total_rows, steps, along_x, c_ref, s_ref, sums_ref, unit_ref, more_ref, *refs):
    out_refs, (g_ref, rep_ref) = refs[:-2], refs[-2:]
    rows, width = g_ref.shape
    block = rows // len(steps)
    here = lax.axis_index("x")
    sums = jnp.sum(sums_ref[...], axis=0)
    for k in range(KNOTS):
        if k == 0:
            cos_off = jnp.full((1, width), total_rows * (1.0 - TARGET[0]), F32)
            sin_total = jnp.zeros((1, width), F32)
        else:
            cos_off = sums[k - 1 : k]
            sin_total = sums[KNOTS + k - 2 : KNOTS + k - 1]
        cos_coef = 2.0 * WEIGHT[k] * (cos_off / total_rows)
        sin_coef = 2.0 * WEIGHT[k] * (sin_total / total_rows)
        rep_ref[k] = jnp.broadcast_to(KNOT[k] * sin_coef, (8, width))
        rep_ref[KNOTS + k] = jnp.broadcast_to(-KNOT[k] * cos_coef, (8, width))

    def tile(i, chip):
        at = pl.ds(pl.multiple_of((i * along_x + chip) * TILE, TILE), TILE)
        c1 = c_ref[at, :].reshape(TILE // 8, 8, width)
        s1 = s_ref[at, :].reshape(TILE // 8, 8, width)
        two = c1 + c1
        a2 = jnp.zeros_like(c1)
        b2 = a2
        a1 = rep_ref[KNOTS - 1] + a2
        b1 = rep_ref[2 * KNOTS - 1] + a2
        for k in range(KNOTS - 2, 0, -1):
            a1, a2 = rep_ref[k] + (two * a1 - a2), a1
            b1, b2 = rep_ref[KNOTS + k] + (two * b1 - b2), b1
        g = rep_ref[0] + (c1 * a1 - a2) + s1 * b1
        return g.reshape(TILE, width).astype(BF16)

    for j, by in enumerate(steps):

        @pl.loop(0, block // TILE)
        def _(i):
            at = pl.ds(pl.multiple_of(j * block + i * TILE, TILE), TILE)
            g_ref[at, :] = tile(i, lax.rem(here + by, along_x))

    step, half = 512, width // 2
    for i in range(unit_ref.shape[0] // step):
        at = pl.ds(i * step, step)
        out = times_transposed(g_ref[:, pl.ds(0, half)], unit_ref[at, :]) + times_transposed(
            g_ref[:, pl.ds(half, half)], more_ref[at, :]
        )
        for j, out_ref in enumerate(out_refs):
            out_ref[:, at] = out[j * block : (j + 1) * block]


def times_transposed(a, b):
    return lax.dot_general(a, b, (((1,), (1,)), ((), ())), preferred_element_type=F32)


def call(kernel, outs, scratch, flops, moved, operands):
    whole = pl.BlockSpec(memory_space=pltpu.VMEM)
    return pl.pallas_call(
        kernel,
        out_shape=outs,
        in_specs=[whole] * operands,
        out_specs=jax.tree.map(lambda _: whole, outs),
        scratch_shapes=scratch,
        compiler_params=pltpu.CompilerParams(vmem_limit_bytes=16 << 20),
        cost_estimate=pl.CostEstimate(flops=flops, bytes_accessed=moved, transcendentals=0),
    )


def to_all(x, axes, peers):
    return lax.all_to_all(jnp.broadcast_to(x[None], (peers,) + x.shape), axes, 0, 0, tiled=True)


def turn(x, axis, by):
    n = lax.axis_size(axis)
    return lax.ppermute(x, axis, [(i, (i + by) % n) for i in range(n)])


def local(embeddings, directions):
    zh, zl, along_x = lax.axis_size("zh"), lax.axis_size("zl"), lax.axis_size("x")
    batch = lax.axis_size("y")
    depth, width = directions.shape
    block = embeddings.shape[0] * zh * zl
    rows = block * along_x
    total_rows = float(2 * rows * batch)
    sds = jax.ShapeDtypeStruct

    theirs = turn(directions, "c", 1)
    units = [
        call(unit_kernel, sds((depth, width), BF16), (), 4 * depth * width, 4 * depth * width, 1)(columns)
        for columns in (directions, theirs)
    ]
    held = to_all(embeddings, "zh", zh).reshape(-1, depth)
    held = to_all(held, ("zl", "x"), zl * along_x).reshape(rows, depth)

    c1, s1, sums = call(
        sums_kernel,
        (sds((rows, 2 * width), F32), sds((rows, 2 * width), F32), sds((2 * KNOTS - 2, 2 * width), F32)),
        (pltpu.VMEM((rows, 2 * width), F32), pltpu.VMEM((2 * KNOTS - 2, 8, 2 * width), F32)),
        4 * rows * depth * width,
        8 * rows * depth,
        3,
    )(held, *units)
    swapped = turn(sums, "c", 1)
    sums = sums + jnp.concatenate([swapped[:, width:], swapped[:, :width]], axis=1)
    sums = to_all(sums.astype(LINK), "y", batch).astype(F32)

    def grad(steps):
        outs = call(
            functools.partial(grad_kernel, total_rows, steps, along_x),
            [sds((block, depth), F32)] * len(steps),
            (pltpu.VMEM((len(steps) * block, 2 * width), BF16), pltpu.VMEM((2 * KNOTS, 8, 2 * width), F32)),
            4 * len(steps) * block * depth * width,
            4 * len(steps) * block * depth,
            5,
        )(c1, s1, sums, *units)
        return dict(zip(steps, outs))

    parts = grad((2, 1, along_x - 1, 0))
    for by in (2, 1, along_x - 1):
        parts[by] = turn(parts[by].astype(LINK), "x", by)
    part = sum(p.astype(F32) for p in parts.values()).astype(LINK)
    part = lax.all_to_all(part.reshape(zl * zh, -1, depth), ("zl", "zh"), 0, 0, tiled=True)
    return jnp.sum(part.astype(F32), axis=0)


def solution(mesh):
    fine = Mesh(mesh.devices.reshape(8, 4, 3, 4, 2), ("y", "zh", "zl", "x", "c"))
    along = ("zh", "zl", "x", "c")
    rows = P(("y",) + along, None)

    return jax.shard_map(local, mesh=fine, in_specs=(rows, P(None, along)), out_specs=rows, check_vma=False)
```

profile of v0, /device:TPU:6, one launch (start us, length us, event | category | flops | bytes accessed | tf_op | source)
XLA Modules:
  0.0 106.6 jit_solution(464819636762945347)
XLA Ops:
  0.0 0.7 broadcast_in_dim.8
  0.7 25.1 %all_to_all.20 = bf16[4,4,2048]{2,1,0:T(4,128)(2,1)S(1)} all-to-all(bf16[4,4,2048]{2,1,0:T(4,128)(2,1)S(1)} %broadcast_in_dim.8), channel_id=1, replica_groups=mesh['y'=8,'zh'=4,'zl'=3,'x'=4,'c'=2] {'zh'}, dimensions={0} | all-to-all | bytes 131072 | tf_op jit(solution)/shard_map/all_to_all | solution.py:148
  25.8 0.0 copy-start
  25.9 1.0 broadcast_in_dim.10
  26.8 5.8 %all-to-all-start.1 = ((bf16[12,16,2048]{2,1,0:T(8,128)(2,1)}), bf16[12,16,2048]{2,1,0:T(8,128)(2,1)S(1)}, u32[]{:S(2)}, u32[]{:S(2)}) async-start(bf16[12,16,2048]{2,1,0:T(8,128)(2,1)} %broadcast_in_dim.10), calls=%async_computation.1 | async-start | bytes 1572864 | tf_op jit(solution)/shard_map/all_to_all | solution.py:148
  32.7 0.0 copy-done
  32.7 1.9 %collective-permute-start = (bf16[2048,256]{1,0:T(8,128)(2,1)S(1)}, bf16[2048,256]{1,0:T(8,128)(2,1)S(1)}, u32[]{:S(2)}, u32[]{:S(2)}) collective-permute-start(bf16[2048,256]{1,0:T(8,128)(2,1)S(1)} %copy-done), channel_id=1, source_target_pairs={{0,1},{1,0},{2,3},{3,2},{4,5},{5,4},{6,7},{7,6},{8,9},{9,8},{10,11... | collective-permute-start | bytes 3145736 | tf_op jit(solution)/shard_map/ppermute | solution.py:153
  34.6 0.3 shard_map.28.unit_ref
  34.9 2.4 %collective-permute-done.dir_ref = bf16[2048,256]{1,0:T(8,128)(2,1)S(1)} collective-permute-done((bf16[2048,256]{1,0:T(8,128)(2,1)S(1)}, bf16[2048,256]{1,0:T(8,128)(2,1)S(1)}, u32[]{:S(2)}, u32[]{:S(2)}) %collective-permute-start) | collective-permute-done | bytes 1048608 | tf_op jit(solution)/shard_map/ppermute | solution.py:153
  37.2 0.3 shard_map.29.more_ref
  37.5 8.4 %all-to-all-done.1 = bf16[12,16,2048]{2,1,0:T(8,128)(2,1)S(1)} async-done(((bf16[12,16,2048]{2,1,0:T(8,128)(2,1)}), bf16[12,16,2048]{2,1,0:T(8,128)(2,1)S(1)}, u32[]{:S(2)}, u32[]{:S(2)}) %all-to-all-start.1) | async-done | bytes 786464 | tf_op jit(solution)/shard_map/all_to_all | solution.py:148
  45.9 2.4 %shard_map.30 = (f32[192,512]{1,0:T(8,128)S(1)}, f32[192,512]{1,0:T(8,128)S(1)}, f32[32,512]{1,0:T(8,128)S(1)}) custom-call(bf16[192,2048]{1,0:T(8,128)(2,1)S(1)} %bitcast.1, bf16[2048,256]{1,0:T(8,128)(2,1)S(1)} %shard_map.28.unit_ref, bf16[2048,256]{1,0:T(8,128)(2,1)S(1)} %shard_map.29.more_ref), custom_call_target="tpu_custom_call" | custom-call | flops 402653184 | bytes 3145728 | tf_op jit(solution)/shard_map/pallas_call | solution.py:173
  48.3 1.9 %collective-permute-start.1 = (f32[32,512]{1,0:T(8,128)S(1)}, f32[32,512]{1,0:T(8,128)S(1)}, u32[]{:S(2)}, u32[]{:S(2)}) collective-permute-start(f32[32,512]{1,0:T(8,128)S(1)} %get-tuple-element.14), channel_id=1, source_target_pairs={{0,1},{1,0},{2,3},{3,2},{4,5},{5,4},{6,7},{7,6},{8,9},{9,8},{10,11... | collective-permute-start | bytes 196616 | tf_op jit(solution)/shard_map/ppermute | solution.py:153
  50.2 1.2 %collective-permute-done.1 = f32[32,512]{1,0:T(8,128)S(1)} collective-permute-done((f32[32,512]{1,0:T(8,128)S(1)}, f32[32,512]{1,0:T(8,128)S(1)}, u32[]{:S(2)}, u32[]{:S(2)}) %collective-permute-start.1) | collective-permute-done | bytes 65568 | tf_op jit(solution)/shard_map/ppermute | solution.py:153
  51.5 19.1 %all_to_all.21 = f16[8,32,512]{2,1,0:T(8,128)(2,1)S(1)} all-to-all(f16[8,32,512]{2,1,0:T(8,128)(2,1)S(1)} %broadcast_in_dim.22), channel_id=1, replica_groups=mesh['y'=8,'zh'=4,'zl'=3,'x'=4,'c'=2] {'y'}, dimensions={0} | all-to-all | bytes 524288 | tf_op jit(solution)/shard_map/all_to_all | solution.py:148
  70.6 0.1 convert_element_type.31.sums_ref
  70.7 2.3 %shard_map.31 = (f32[48,2048]{1,0:T(8,128)S(1)}, f32[48,2048]{1,0:T(8,128)S(1)}, f32[48,2048]{1,0:T(8,128)S(1)}, f32[48,2048]{1,0:T(8,128)S(1)}) custom-call(f32[192,512]{1,0:T(8,128)S(1)} %get-tuple-element.12.c_ref, f32[192,512]{1,0:T(8,128)S(1)} %get-tuple-element.13.s_ref, f32[8,32,512]{2,1,0:T(8,128)S(1)} %convert_element_type.31.sums_ref, ...), custom_call_target="tpu_custom_call" | custom-call | flops 402653184 | bytes 1572864 | tf_op jit(solution)/shard_map/pallas_call | solution.py:186
  73.0 1.9 %collective-permute-start.4 = (f16[48,2048]{1,0:T(8,128)(2,1)S(1)}, f16[48,2048]{1,0:T(8,128)(2,1)S(1)}, u32[]{:S(2)}, u32[]{:S(2)}) collective-permute-start(f16[48,2048]{1,0:T(8,128)(2,1)S(1)} %convert_element_type.36), channel_id=1, source_target_pairs={{0,6},{2,0},{4,2},{6,4},{1,7},{3,1},{5,3},{7,5},{8,14},{10,8},{12,... | collective-permute-start | bytes 589832 | tf_op jit(solution)/shard_map/ppermute | solution.py:153
  75.0 5.1 %collective-permute-start.3 = (f16[48,2048]{1,0:T(8,128)(2,1)S(1)}, f16[48,2048]{1,0:T(8,128)(2,1)S(1)}, u32[]{:S(2)}, u32[]{:S(2)}) collective-permute-start(f16[48,2048]{1,0:T(8,128)(2,1)S(1)} %convert_element_type.34), channel_id=1, source_target_pairs={{0,2},{2,4},{4,6},{6,0},{1,3},{3,5},{5,7},{7,1},{8,10},{10,12},{12... | collective-permute-start | bytes 589832 | tf_op jit(solution)/shard_map/ppermute | solution.py:153
  80.1 1.9 %collective-permute-start.2 = (f16[48,2048]{1,0:T(8,128)(2,1)S(1)}, f16[48,2048]{1,0:T(8,128)(2,1)S(1)}, u32[]{:S(2)}, u32[]{:S(2)}) collective-permute-start(f16[48,2048]{1,0:T(8,128)(2,1)S(1)} %convert_element_type.32), channel_id=1, source_target_pairs={{0,4},{2,6},{4,0},{6,2},{1,5},{3,7},{5,1},{7,3},{8,12},{10,14},{12... | collective-permute-start | bytes 589832 | tf_op jit(solution)/shard_map/ppermute | solution.py:153
  82.0 0.0 collective-permute-done.4
  82.1 5.4 %collective-permute-done.3 = f16[48,2048]{1,0:T(8,128)(2,1)S(1)} collective-permute-done((f16[48,2048]{1,0:T(8,128)(2,1)S(1)}, f16[48,2048]{1,0:T(8,128)(2,1)S(1)}, u32[]{:S(2)}, u32[]{:S(2)}) %collective-permute-start.3) | collective-permute-done | bytes 196640 | tf_op jit(solution)/shard_map/ppermute | solution.py:153
  87.4 1.7 %collective-permute-done.2 = f16[48,2048]{1,0:T(8,128)(2,1)S(1)} collective-permute-done((f16[48,2048]{1,0:T(8,128)(2,1)S(1)}, f16[48,2048]{1,0:T(8,128)(2,1)S(1)}, u32[]{:S(2)}, u32[]{:S(2)}) %collective-permute-start.2) | collective-permute-done | bytes 196640 | tf_op jit(solution)/shard_map/ppermute | solution.py:153
  89.2 0.1 add_convert_fusion
  89.3 0.1 reshape.10
  89.4 16.5 %all_to_all.22 = f16[12,4,2048]{2,1,0:T(4,128)(2,1)S(1)} all-to-all(f16[12,4,2048]{2,1,0:T(4,128)(2,1)S(1)} %reshape.10), channel_id=1, replica_groups=mesh['y'=8,'zh'=4,'zl'=3,'x'=4,'c'=2] {'zl','zh'}, dimensions={0} | all-to-all | bytes 393216 | tf_op jit(solution)/shard_map/all_to_all | solution.py:200
  105.9 0.7 convert_reduce_fusion
  (7 shorter events, 0.1 us)
Async XLA Ops:
  25.8 6.8 %copy-start = (bf16[2048,256]{1,0:T(8,128)(2,1)S(1)}, bf16[2048,256]{1,0:T(8,128)(2,1)}, u32[]{:S(2)}) copy-start(bf16[2048,256]{1,0:T(8,128)(2,1)} %dir_ref.1) | copy-start | bytes 3145732
  26.8 19.1 %all-to-all-start.1 = ((bf16[12,16,2048]{2,1,0:T(8,128)(2,1)}), bf16[12,16,2048]{2,1,0:T(8,128)(2,1)S(1)}, u32[]{:S(2)}, u32[]{:S(2)}) async-start(bf16[12,16,2048]{2,1,0:T(8,128)(2,1)} %broadcast_in_dim.10), calls=%async_computation.1 | async-start | bytes 1572864 | tf_op jit(solution)/shard_map/all_to_all | solution.py:148
  32.7 4.5 %collective-permute-start = (bf16[2048,256]{1,0:T(8,128)(2,1)S(1)}, bf16[2048,256]{1,0:T(8,128)(2,1)S(1)}, u32[]{:S(2)}, u32[]{:S(2)}) collective-permute-start(bf16[2048,256]{1,0:T(8,128)(2,1)S(1)} %copy-done), channel_id=1, source_target_pairs={{0,1},{1,0},{2,3},{3,2},{4,5},{5,4},{6,7},{7,6},{8,9},{9,8},{10,11... | collective-permute-start | bytes 3145736 | tf_op jit(solution)/shard_map/ppermute | solution.py:153
  48.3 3.1 %collective-permute-start.1 = (f32[32,512]{1,0:T(8,128)S(1)}, f32[32,512]{1,0:T(8,128)S(1)}, u32[]{:S(2)}, u32[]{:S(2)}) collective-permute-start(f32[32,512]{1,0:T(8,128)S(1)} %get-tuple-element.14), channel_id=1, source_target_pairs={{0,1},{1,0},{2,3},{3,2},{4,5},{5,4},{6,7},{7,6},{8,9},{9,8},{10,11... | collective-permute-start | bytes 196616 | tf_op jit(solution)/shard_map/ppermute | solution.py:153
  73.0 9.0 %collective-permute-start.4 = (f16[48,2048]{1,0:T(8,128)(2,1)S(1)}, f16[48,2048]{1,0:T(8,128)(2,1)S(1)}, u32[]{:S(2)}, u32[]{:S(2)}) collective-permute-start(f16[48,2048]{1,0:T(8,128)(2,1)S(1)} %convert_element_type.36), channel_id=1, source_target_pairs={{0,6},{2,0},{4,2},{6,4},{1,7},{3,1},{5,3},{7,5},{8,14},{10,8},{12,... | collective-permute-start | bytes 589832 | tf_op jit(solution)/shard_map/ppermute | solution.py:153
  75.0 12.5 %collective-permute-start.3 = (f16[48,2048]{1,0:T(8,128)(2,1)S(1)}, f16[48,2048]{1,0:T(8,128)(2,1)S(1)}, u32[]{:S(2)}, u32[]{:S(2)}) collective-permute-start(f16[48,2048]{1,0:T(8,128)(2,1)S(1)} %convert_element_type.34), channel_id=1, source_target_pairs={{0,2},{2,4},{4,6},{6,0},{1,3},{3,5},{5,7},{7,1},{8,10},{10,12},{12... | collective-permute-start | bytes 589832 | tf_op jit(solution)/shard_map/ppermute | solution.py:153
  80.1 9.1 %collective-permute-start.2 = (f16[48,2048]{1,0:T(8,128)(2,1)S(1)}, f16[48,2048]{1,0:T(8,128)(2,1)S(1)}, u32[]{:S(2)}, u32[]{:S(2)}) collective-permute-start(f16[48,2048]{1,0:T(8,128)(2,1)S(1)} %convert_element_type.32), channel_id=1, source_target_pairs={{0,4},{2,6},{4,0},{6,2},{1,5},{3,7},{5,1},{7,3},{8,12},{10,14},{12... | collective-permute-start | bytes 589832 | tf_op jit(solution)/shard_map/ppermute | solution.py:153
where the time goes:
time: 107 us
  blocking collectives  60.7 us (57%)
  waiting for transfers between devices  19.1 us (18%)
  starting transfers between devices  18.7 us (17%)
  Pallas kernels  5.19 us (5%)
  local copies, waits for them, and re-layouts  1.85 us (2%)
    all_to_all x2, blocking collectives, to_all(): lax.all_to_all(jnp.broadcast_to(x[None], (peers,) + x.shape), axes, 0, 0,...  44.2 us
    all_to_all x1, blocking collectives, local(): lax.all_to_all(part.reshape(zl * zh, -1, depth), ('zl', 'zh'), 0, 0, tile...  16.5 us
    ppermute x5, starting transfers between devices, turn(): return lax.ppermute(x, axis, [(i, (i + by) % n) for i in range(n)])  12.8 us
    ppermute x5, waiting for transfers between devices, turn(): return lax.ppermute(x, axis, [(i, (i + by) % n) for i in range(n)])  10.7 us
    all_to_all x1, waiting for transfers between devices, to_all(): lax.all_to_all(jnp.broadcast_to(x[None], (peers,) + x.shape), axes, 0, 0,...  8.41 us
    all_to_all x1, starting transfers between devices, to_all(): lax.all_to_all(jnp.broadcast_to(x[None], (peers,) + x.shape), axes, 0, 0,...  5.85 us
    pallas_call x1, Pallas kernels, local(): call(sums_kernel, (sds((rows, 2 * width), F32), sds((rows, 2 * width), F3...  2.4 us
    pallas_call x1, Pallas kernels, grad(): call(functools.partial(grad_kernel, total_rows, steps, along_x), [sds((bl...  2.27 us
  transfers between devices with their start and end apart: 6, of which 5 were waited for; matrix products, arithmetic and copies ran while one was open for 0% of the time, Pallas kernels for 0%

commit v1 on v0

--- a/solution.py
+++ b/solution.py
@@ -81,7 +81,6 @@
     out_refs, (g_ref, rep_ref) = refs[:-2], refs[-2:]
     rows, width = g_ref.shape
     block = rows // len(steps)
-    here = lax.axis_index("x")
     sums = jnp.sum(sums_ref[...], axis=0)
     for k in range(KNOTS):
         if k == 0:
@@ -115,7 +114,7 @@
         @pl.loop(0, block // TILE)
         def _(i):
             at = pl.ds(pl.multiple_of(j * block + i * TILE, TILE), TILE)
-            g_ref[at, :] = tile(i, lax.rem(here + by, along_x))
+            g_ref[at, :] = tile(i, by)
 
     step, half = 512, width // 2
     for i in range(unit_ref.shape[0] // step):
@@ -123,8 +122,7 @@
         out = times_transposed(g_ref[:, pl.ds(0, half)], unit_ref[at, :]) + times_transposed(
             g_ref[:, pl.ds(half, half)], more_ref[at, :]
         )
-        for j, out_ref in enumerate(out_refs):
-            out_ref[:, at] = out[j * block : (j + 1) * block]
+        out_refs[0][:, at] = out
 
 
 def times_transposed(a, b):
@@ -162,13 +160,16 @@
     total_rows = float(2 * rows * batch)
     sds = jax.ShapeDtypeStruct
 
-    theirs = turn(directions, "c", 1)
+    with jax.named_scope("columns"):
+        theirs = turn(directions, "c", 1)
     units = [
         call(unit_kernel, sds((depth, width), BF16), (), 4 * depth * width, 4 * depth * width, 1)(columns)
         for columns in (directions, theirs)
     ]
-    held = to_all(embeddings, "zh", zh).reshape(-1, depth)
-    held = to_all(held, ("zl", "x"), zl * along_x).reshape(rows, depth)
+    with jax.named_scope("far"):
+        held = to_all(embeddings, "zh", zh).reshape(-1, depth)
+    with jax.named_scope("near"):
+        held = to_all(held, ("zl", "x"), zl * along_x).reshape(rows, depth)
 
     c1, s1, sums = call(
         sums_kernel,
@@ -182,21 +183,16 @@
     sums = sums + jnp.concatenate([swapped[:, width:], swapped[:, :width]], axis=1)
     sums = to_all(sums.astype(LINK), "y", batch).astype(F32)
 
-    def grad(steps):
-        outs = call(
-            functools.partial(grad_kernel, total_rows, steps, along_x),
-            [sds((block, depth), F32)] * len(steps),
-            (pltpu.VMEM((len(steps) * block, 2 * width), BF16), pltpu.VMEM((2 * KNOTS, 8, 2 * width), F32)),
-            4 * len(steps) * block * depth * width,
-            4 * len(steps) * block * depth,
-            5,
-        )(c1, s1, sums, *units)
-        return dict(zip(steps, outs))
-
-    parts = grad((2, 1, along_x - 1, 0))
-    for by in (2, 1, along_x - 1):
-        parts[by] = turn(parts[by].astype(LINK), "x", by)
-    part = sum(p.astype(F32) for p in parts.values()).astype(LINK)
+    part = call(
+        functools.partial(grad_kernel, total_rows, tuple(range(along_x)), along_x),
+        sds((rows, depth), F32),
+        (pltpu.VMEM((rows, 2 * width), BF16), pltpu.VMEM((2 * KNOTS, 8, 2 * width), F32)),
+        4 * rows * depth * width,
+        4 * rows * depth,
+        5,
+    )(c1, s1, sums, *units)
+    part = lax.all_to_all(part.astype(LINK).reshape(along_x, block, depth), "x", 0, 0, tiled=True)
+    part = jnp.sum(part.astype(F32), axis=0).astype(LINK)
     part = lax.all_to_all(part.reshape(zl * zh, -1, depth), ("zl", "zh"), 0, 0, tiled=True)
     return jnp.sum(part.astype(F32), axis=0)
 

time: 107 us -> 106 us (level)
  blocking collectives: 60.7 us -> 75.3 us
  starting transfers between devices: 18.7 us -> 9.68 us
  waiting for transfers between devices: 19.1 us -> 12 us
    all_to_all x0 -> x1, blocking collectives: none -> 13.6 us  [local(): lax.all_to_all(part.astype(LINK).reshape(along_x, block, depth), 'x', 0,...]
    ppermute x5 -> x2, starting transfers between devices: 12.8 us -> 3.84 us  [turn(): return lax.ppermute(x, axis, [(i, (i + by) % n) for i in range(n)])]
    ppermute x5 -> x2, waiting for transfers between devices: 10.7 us -> 3.58 us  [turn(): return lax.ppermute(x, axis, [(i, (i + by) % n) for i in range(n)])]
  transfers between devices with their start and end apart: 6 -> 3, of which waited for: 5 -> 3; matrix products, arithmetic and copies ran while one was open for 0% -> 0% of each run, Pallas kernels for 0% -> 0%
where the time goes in v1:
time: 106 us; the launch traced here: 105 us
  blocking collectives  75.3 us (71%)
  waiting for transfers between devices  12 us (11%)
  starting transfers between devices  9.68 us (9%)
  Pallas kernels  5.21 us (5%)
  local copies, waits for them, and re-layouts  1.93 us (2%)
    all_to_all x2, blocking collectives, to_all(): lax.all_to_all(jnp.broadcast_to(x[None], (peers,) + x.shape), axes, 0, 0,...  44.2 us
    all_to_all x1, blocking collectives, local(): lax.all_to_all(part.reshape(zl * zh, -1, depth), ('zl', 'zh'), 0, 0, tile...  17.6 us
    all_to_all x1, blocking collectives, local(): lax.all_to_all(part.astype(LINK).reshape(along_x, block, depth), 'x', 0,...  13.6 us
    all_to_all x1, waiting for transfers between devices, to_all(): lax.all_to_all(jnp.broadcast_to(x[None], (peers,) + x.shape), axes, 0, 0,...  8.41 us
    all_to_all x1, starting transfers between devices, to_all(): lax.all_to_all(jnp.broadcast_to(x[None], (peers,) + x.shape), axes, 0, 0,...  5.85 us
    ppermute x2, starting transfers between devices, turn(): return lax.ppermute(x, axis, [(i, (i + by) % n) for i in range(n)])  3.84 us
    ppermute x2, waiting for transfers between devices, turn(): return lax.ppermute(x, axis, [(i, (i + by) % n) for i in range(n)])  3.58 us
    pallas_call x1, Pallas kernels, local(): call(sums_kernel, (sds((rows, 2 * width), F32), sds((rows, 2 * width), F3...  2.4 us
  transfers between devices with their start and end apart: 3, of which 3 were waited for; matrix products, arithmetic and copies ran while one was open for 0% of the time, Pallas kernels for 0%

profile of v1, /device:TPU:6, one launch (start us, length us, event | category | flops | bytes accessed | tf_op | source)
XLA Modules:
  0.0 105.2 jit_solution(478701969759428366)
XLA Ops:
  0.0 0.0 copy-start
  0.0 0.8 broadcast_in_dim.8
  0.8 25.1 %all_to_all.25 = bf16[4,4,2048]{2,1,0:T(4,128)(2,1)S(1)} all-to-all(bf16[4,4,2048]{2,1,0:T(4,128)(2,1)S(1)} %broadcast_in_dim.8), channel_id=1, replica_groups=mesh['y'=8,'zh'=4,'zl'=3,'x'=4,'c'=2] {'zh'}, dimensions={0} | all-to-all | bytes 131072 | tf_op jit(solution)/shard_map/far/all_to_all | solution.py:146
  25.9 1.0 broadcast_in_dim.10
  26.9 5.8 %all-to-all-start.1 = ((bf16[12,16,2048]{2,1,0:T(8,128)(2,1)}), bf16[12,16,2048]{2,1,0:T(8,128)(2,1)S(1)}, u32[]{:S(2)}, u32[]{:S(2)}) async-start(bf16[12,16,2048]{2,1,0:T(8,128)(2,1)} %broadcast_in_dim.10), calls=%async_computation.1 | async-start | bytes 1572864 | tf_op jit(solution)/shard_map/near/all_to_all | solution.py:146
  32.8 0.0 copy-done
  32.8 1.9 %collective-permute-start = (bf16[2048,256]{1,0:T(8,128)(2,1)S(1)}, bf16[2048,256]{1,0:T(8,128)(2,1)S(1)}, u32[]{:S(2)}, u32[]{:S(2)}) collective-permute-start(bf16[2048,256]{1,0:T(8,128)(2,1)S(1)} %copy-done), channel_id=1, source_target_pairs={{0,1},{1,0},{2,3},{3,2},{4,5},{5,4},{6,7},{7,6},{8,9},{9,8},{10,11... | collective-permute-start | bytes 3145736 | tf_op jit(solution)/shard_map/columns/ppermute | solution.py:151
  34.7 0.3 shard_map.28.unit_ref
  34.9 2.4 %collective-permute-done.dir_ref = bf16[2048,256]{1,0:T(8,128)(2,1)S(1)} collective-permute-done((bf16[2048,256]{1,0:T(8,128)(2,1)S(1)}, bf16[2048,256]{1,0:T(8,128)(2,1)S(1)}, u32[]{:S(2)}, u32[]{:S(2)}) %collective-permute-start) | collective-permute-done | bytes 1048608 | tf_op jit(solution)/shard_map/columns/ppermute | solution.py:151
  37.3 0.3 shard_map.29.more_ref
  37.6 8.4 %all-to-all-done.1 = bf16[12,16,2048]{2,1,0:T(8,128)(2,1)S(1)} async-done(((bf16[12,16,2048]{2,1,0:T(8,128)(2,1)}), bf16[12,16,2048]{2,1,0:T(8,128)(2,1)S(1)}, u32[]{:S(2)}, u32[]{:S(2)}) %all-to-all-start.1) | async-done | bytes 786464 | tf_op jit(solution)/shard_map/near/all_to_all | solution.py:146
  46.0 2.4 %shard_map.30 = (f32[192,512]{1,0:T(8,128)S(1)}, f32[192,512]{1,0:T(8,128)S(1)}, f32[32,512]{1,0:T(8,128)S(1)}) custom-call(bf16[192,2048]{1,0:T(8,128)(2,1)S(1)} %bitcast.2, bf16[2048,256]{1,0:T(8,128)(2,1)S(1)} %shard_map.28.unit_ref, bf16[2048,256]{1,0:T(8,128)(2,1)S(1)} %shard_map.29.more_ref), custom_call_target="tpu_custom_call" | custom-call | flops 402653184 | bytes 3145728 | tf_op jit(solution)/shard_map/pallas_call | solution.py:174
  48.4 1.9 %collective-permute-start.1 = (f32[32,512]{1,0:T(8,128)S(1)}, f32[32,512]{1,0:T(8,128)S(1)}, u32[]{:S(2)}, u32[]{:S(2)}) collective-permute-start(f32[32,512]{1,0:T(8,128)S(1)} %get-tuple-element.10), channel_id=1, source_target_pairs={{0,1},{1,0},{2,3},{3,2},{4,5},{5,4},{6,7},{7,6},{8,9},{9,8},{10,11... | collective-permute-start | bytes 196616 | tf_op jit(solution)/shard_map/ppermute | solution.py:151
  50.3 1.2 %collective-permute-done.1 = f32[32,512]{1,0:T(8,128)S(1)} collective-permute-done((f32[32,512]{1,0:T(8,128)S(1)}, f32[32,512]{1,0:T(8,128)S(1)}, u32[]{:S(2)}, u32[]{:S(2)}) %collective-permute-start.1) | collective-permute-done | bytes 65568 | tf_op jit(solution)/shard_map/ppermute | solution.py:151
  51.6 19.1 %all_to_all.26 = f16[8,32,512]{2,1,0:T(8,128)(2,1)S(1)} all-to-all(f16[8,32,512]{2,1,0:T(8,128)(2,1)S(1)} %broadcast_in_dim.22), channel_id=1, replica_groups=mesh['y'=8,'zh'=4,'zl'=3,'x'=4,'c'=2] {'y'}, dimensions={0} | all-to-all | bytes 524288 | tf_op jit(solution)/shard_map/all_to_all | solution.py:146
  70.7 0.1 convert_element_type.23.sums_ref
  70.7 2.3 %shard_map.31 = f32[192,2048]{1,0:T(8,128)S(1)} custom-call(f32[192,512]{1,0:T(8,128)S(1)} %get-tuple-element.8.c_ref, f32[192,512]{1,0:T(8,128)S(1)} %get-tuple-element.9.s_ref, f32[8,32,512]{2,1,0:T(8,128)S(1)} %convert_element_type.23.sums_ref, bf16[2048,256]{1,0:T(8,128)(2,1)S(1)} %shard_map.28.unit_ref, bf16[2048,256]{1,0:T(8,128)(2,1)S(1)} %shard_map.29.more_ref), custom_call_target="tpu_custom_call" | custom-call | flops 402653184 | bytes 1572864 | tf_op jit(solution)/shard_map/pallas_call | solution.py:186
  73.0 0.1 convert_element_type.24
  73.2 13.6 %all_to_all.27 = f16[4,48,2048]{2,1,0:T(8,128)(2,1)S(1)} all-to-all(f16[4,48,2048]{2,1,0:T(8,128)(2,1)S(1)} %bitcast.3), channel_id=1, replica_groups=mesh['y'=8,'zh'=4,'zl'=3,'x'=4,'c'=2] {'x'}, dimensions={0} | all-to-all | bytes 1572864 | tf_op jit(solution)/shard_map/all_to_all | solution.py:194
  86.7 0.1 convert_reduce_fusion
  86.9 0.1 convert_element_type.27
  87.0 17.6 %all_to_all.28 = f16[12,4,2048]{2,1,0:T(4,128)(2,1)S(1)} all-to-all(f16[12,4,2048]{2,1,0:T(4,128)(2,1)S(1)} %convert_element_type.27), channel_id=1, replica_groups=mesh['y'=8,'zh'=4,'zl'=3,'x'=4,'c'=2] {'zl','zh'}, dimensions={0} | all-to-all | bytes 393216 | tf_op jit(solution)/shard_map/all_to_all | solution.py:196
  104.5 0.7 convert_reduce_fusion.1
  (5 shorter events, 0.1 us)
Async XLA Ops:
  0.0 32.8 %copy-start = (bf16[2048,256]{1,0:T(8,128)(2,1)S(1)}, bf16[2048,256]{1,0:T(8,128)(2,1)}, u32[]{:S(2)}) copy-start(bf16[2048,256]{1,0:T(8,128)(2,1)} %dir_ref.1) | copy-start | bytes 3145732
  26.9 19.1 %all-to-all-start.1 = ((bf16[12,16,2048]{2,1,0:T(8,128)(2,1)}), bf16[12,16,2048]{2,1,0:T(8,128)(2,1)S(1)}, u32[]{:S(2)}, u32[]{:S(2)}) async-start(bf16[12,16,2048]{2,1,0:T(8,128)(2,1)} %broadcast_in_dim.10), calls=%async_computation.1 | async-start | bytes 1572864 | tf_op jit(solution)/shard_map/near/all_to_all | solution.py:146
  32.8 4.5 %collective-permute-start = (bf16[2048,256]{1,0:T(8,128)(2,1)S(1)}, bf16[2048,256]{1,0:T(8,128)(2,1)S(1)}, u32[]{:S(2)}, u32[]{:S(2)}) collective-permute-start(bf16[2048,256]{1,0:T(8,128)(2,1)S(1)} %copy-done), channel_id=1, source_target_pairs={{0,1},{1,0},{2,3},{3,2},{4,5},{5,4},{6,7},{7,6},{8,9},{9,8},{10,11... | collective-permute-start | bytes 3145736 | tf_op jit(solution)/shard_map/columns/ppermute | solution.py:151
  48.4 3.1 %collective-permute-start.1 = (f32[32,512]{1,0:T(8,128)S(1)}, f32[32,512]{1,0:T(8,128)S(1)}, u32[]{:S(2)}, u32[]{:S(2)}) collective-permute-start(f32[32,512]{1,0:T(8,128)S(1)} %get-tuple-element.10), channel_id=1, source_target_pairs={{0,1},{1,0},{2,3},{3,2},{4,5},{5,4},{6,7},{7,6},{8,9},{9,8},{10,11... | collective-permute-start | bytes 196616 | tf_op jit(solution)/shard_map/ppermute | solution.py:151

commit v2 on v1

--- a/solution.py
+++ b/solution.py
@@ -77,10 +77,9 @@
         out_ref[pl.ds(k - 1, 1), :] -= rows * TARGET[k]
 
 
-def grad_kernel(total_rows, steps, along_x, c_ref, s_ref, sums_ref, unit_ref, more_ref, *refs):
+def grad_kernel(total_rows, c_ref, s_ref, sums_ref, unit_ref, more_ref, *refs):
     out_refs, (g_ref, rep_ref) = refs[:-2], refs[-2:]
     rows, width = g_ref.shape
-    block = rows // len(steps)
     sums = jnp.sum(sums_ref[...], axis=0)
     for k in range(KNOTS):
         if k == 0:
@@ -94,8 +93,8 @@
         rep_ref[k] = jnp.broadcast_to(KNOT[k] * sin_coef, (8, width))
         rep_ref[KNOTS + k] = jnp.broadcast_to(-KNOT[k] * cos_coef, (8, width))
 
-    def tile(i, chip):
-        at = pl.ds(pl.multiple_of((i * along_x + chip) * TILE, TILE), TILE)
+    def tile(i):
+        at = pl.ds(pl.multiple_of(i * TILE, TILE), TILE)
         c1 = c_ref[at, :].reshape(TILE // 8, 8, width)
         s1 = s_ref[at, :].reshape(TILE // 8, 8, width)
         two = c1 + c1
@@ -109,12 +108,9 @@
         g = rep_ref[0] + (c1 * a1 - a2) + s1 * b1
         return g.reshape(TILE, width).astype(BF16)
 
-    for j, by in enumerate(steps):
-
-        @pl.loop(0, block // TILE)
-        def _(i):
-            at = pl.ds(pl.multiple_of(j * block + i * TILE, TILE), TILE)
-            g_ref[at, :] = tile(i, by)
+    @pl.loop(0, rows // TILE)
+    def _(i):
+        g_ref[pl.ds(pl.multiple_of(i * TILE, TILE), TILE), :] = tile(i)
 
     step, half = 512, width // 2
     for i in range(unit_ref.shape[0] // step):
@@ -184,16 +180,16 @@
     sums = to_all(sums.astype(LINK), "y", batch).astype(F32)
 
     part = call(
-        functools.partial(grad_kernel, total_rows, tuple(range(along_x)), along_x),
+        functools.partial(grad_kernel, total_rows),
         sds((rows, depth), F32),
         (pltpu.VMEM((rows, 2 * width), BF16), pltpu.VMEM((2 * KNOTS, 8, 2 * width), F32)),
         4 * rows * depth * width,
         4 * rows * depth,
         5,
     )(c1, s1, sums, *units)
-    part = lax.all_to_all(part.astype(LINK).reshape(along_x, block, depth), "x", 0, 0, tiled=True)
-    part = jnp.sum(part.astype(F32), axis=0).astype(LINK)
-    part = lax.all_to_all(part.reshape(zl * zh, -1, depth), ("zl", "zh"), 0, 0, tiled=True)
+    part = lax.all_to_all(part.astype(LINK).reshape(zl * along_x, -1, depth), ("zl", "x"), 0, 0, tiled=True)
+    part = jnp.sum(part.astype(F32), axis=0).astype(LINK).reshape(zh, -1, depth)
+    part = lax.all_to_all(part, "zh", 0, 0, tiled=True)
     return jnp.sum(part.astype(F32), axis=0)
 
 

time: 106 us -> 109 us (1.028)
  blocking collectives: 75.3 us -> 78.2 us
    all_to_all x2, blocking collectives: 31.1 us -> 34.1 us  [the longest x1 18.4 us: local(): lax.all_to_all(part.astype(LINK).reshape(zl * along_x, -1, depth), ('zl',...]
where the time goes in v2:
time: 109 us; the launch traced here: 108 us
  blocking collectives  78.2 us (72%)
  waiting for transfers between devices  12 us (11%)
  starting transfers between devices  9.68 us (9%)
  Pallas kernels  5.21 us (5%)
  local copies, waits for them, and re-layouts  1.88 us (2%)
    all_to_all x2, blocking collectives, to_all(): lax.all_to_all(jnp.broadcast_to(x[None], (peers,) + x.shape), axes, 0, 0,...  44.2 us
    all_to_all x1, blocking collectives, local(): lax.all_to_all(part.astype(LINK).reshape(zl * along_x, -1, depth), ('zl',...  18.4 us
    all_to_all x1, blocking collectives, local(): part = lax.all_to_all(part, 'zh', 0, 0, tiled=True)  15.7 us
    all_to_all x1, waiting for transfers between devices, to_all(): lax.all_to_all(jnp.broadcast_to(x[None], (peers,) + x.shape), axes, 0, 0,...  8.41 us
    all_to_all x1, starting transfers between devices, to_all(): lax.all_to_all(jnp.broadcast_to(x[None], (peers,) + x.shape), axes, 0, 0,...  5.85 us
    ppermute x2, starting transfers between devices, turn(): return lax.ppermute(x, axis, [(i, (i + by) % n) for i in range(n)])  3.84 us
    ppermute x2, waiting for transfers between devices, turn(): return lax.ppermute(x, axis, [(i, (i + by) % n) for i in range(n)])  3.58 us
    pallas_call x1, Pallas kernels, local(): call(sums_kernel, (sds((rows, 2 * width), F32), sds((rows, 2 * width), F3...  2.4 us
  transfers between devices with their start and end apart: 3, of which 3 were waited for; matrix products, arithmetic and copies ran while one was open for 0% of the time, Pallas kernels for 0%

profile of v2, /device:TPU:6, one launch (start us, length us, event | category | flops | bytes accessed | tf_op | source)
XLA Modules:
  0.0 108.0 jit_solution(8181322216176621010)
XLA Ops:
  0.0 0.0 copy-start
  0.0 0.8 broadcast_in_dim.8
  0.8 25.1 %all_to_all.25 = bf16[4,4,2048]{2,1,0:T(4,128)(2,1)S(1)} all-to-all(bf16[4,4,2048]{2,1,0:T(4,128)(2,1)S(1)} %broadcast_in_dim.8), channel_id=1, replica_groups=mesh['y'=8,'zh'=4,'zl'=3,'x'=4,'c'=2] {'zh'}, dimensions={0} | all-to-all | bytes 131072 | tf_op jit(solution)/shard_map/far/all_to_all | solution.py:142
  25.9 1.0 broadcast_in_dim.10
  26.9 5.8 %all-to-all-start.1 = ((bf16[12,16,2048]{2,1,0:T(8,128)(2,1)}), bf16[12,16,2048]{2,1,0:T(8,128)(2,1)S(1)}, u32[]{:S(2)}, u32[]{:S(2)}) async-start(bf16[12,16,2048]{2,1,0:T(8,128)(2,1)} %broadcast_in_dim.10), calls=%async_computation.1 | async-start | bytes 1572864 | tf_op jit(solution)/shard_map/near/all_to_all | solution.py:142
  32.8 0.0 copy-done
  32.8 1.9 %collective-permute-start = (bf16[2048,256]{1,0:T(8,128)(2,1)S(1)}, bf16[2048,256]{1,0:T(8,128)(2,1)S(1)}, u32[]{:S(2)}, u32[]{:S(2)}) collective-permute-start(bf16[2048,256]{1,0:T(8,128)(2,1)S(1)} %copy-done), channel_id=1, source_target_pairs={{0,1},{1,0},{2,3},{3,2},{4,5},{5,4},{6,7},{7,6},{8,9},{9,8},{10,11... | collective-permute-start | bytes 3145736 | tf_op jit(solution)/shard_map/columns/ppermute | solution.py:147
  34.7 0.3 shard_map.28.unit_ref
  34.9 2.4 %collective-permute-done.dir_ref = bf16[2048,256]{1,0:T(8,128)(2,1)S(1)} collective-permute-done((bf16[2048,256]{1,0:T(8,128)(2,1)S(1)}, bf16[2048,256]{1,0:T(8,128)(2,1)S(1)}, u32[]{:S(2)}, u32[]{:S(2)}) %collective-permute-start) | collective-permute-done | bytes 1048608 | tf_op jit(solution)/shard_map/columns/ppermute | solution.py:147
  37.3 0.3 shard_map.29.more_ref
  37.6 8.4 %all-to-all-done.1 = bf16[12,16,2048]{2,1,0:T(8,128)(2,1)S(1)} async-done(((bf16[12,16,2048]{2,1,0:T(8,128)(2,1)}), bf16[12,16,2048]{2,1,0:T(8,128)(2,1)S(1)}, u32[]{:S(2)}, u32[]{:S(2)}) %all-to-all-start.1) | async-done | bytes 786464 | tf_op jit(solution)/shard_map/near/all_to_all | solution.py:142
  46.0 2.4 %shard_map.30 = (f32[192,512]{1,0:T(8,128)S(1)}, f32[192,512]{1,0:T(8,128)S(1)}, f32[32,512]{1,0:T(8,128)S(1)}) custom-call(bf16[192,2048]{1,0:T(8,128)(2,1)S(1)} %bitcast.2, bf16[2048,256]{1,0:T(8,128)(2,1)S(1)} %shard_map.28.unit_ref, bf16[2048,256]{1,0:T(8,128)(2,1)S(1)} %shard_map.29.more_ref), custom_call_target="tpu_custom_call" | custom-call | flops 402653184 | bytes 3145728 | tf_op jit(solution)/shard_map/pallas_call | solution.py:170
  48.4 1.9 %collective-permute-start.1 = (f32[32,512]{1,0:T(8,128)S(1)}, f32[32,512]{1,0:T(8,128)S(1)}, u32[]{:S(2)}, u32[]{:S(2)}) collective-permute-start(f32[32,512]{1,0:T(8,128)S(1)} %get-tuple-element.10), channel_id=1, source_target_pairs={{0,1},{1,0},{2,3},{3,2},{4,5},{5,4},{6,7},{7,6},{8,9},{9,8},{10,11... | collective-permute-start | bytes 196616 | tf_op jit(solution)/shard_map/ppermute | solution.py:147
  50.3 1.2 %collective-permute-done.1 = f32[32,512]{1,0:T(8,128)S(1)} collective-permute-done((f32[32,512]{1,0:T(8,128)S(1)}, f32[32,512]{1,0:T(8,128)S(1)}, u32[]{:S(2)}, u32[]{:S(2)}) %collective-permute-start.1) | collective-permute-done | bytes 65568 | tf_op jit(solution)/shard_map/ppermute | solution.py:147
  51.6 19.1 %all_to_all.26 = f16[8,32,512]{2,1,0:T(8,128)(2,1)S(1)} all-to-all(f16[8,32,512]{2,1,0:T(8,128)(2,1)S(1)} %broadcast_in_dim.22), channel_id=1, replica_groups=mesh['y'=8,'zh'=4,'zl'=3,'x'=4,'c'=2] {'y'}, dimensions={0} | all-to-all | bytes 524288 | tf_op jit(solution)/shard_map/all_to_all | solution.py:142
  70.7 0.1 convert_element_type.23.sums_ref
  70.7 2.3 %shard_map.31 = f32[192,2048]{1,0:T(8,128)S(1)} custom-call(f32[192,512]{1,0:T(8,128)S(1)} %get-tuple-element.8.c_ref, f32[192,512]{1,0:T(8,128)S(1)} %get-tuple-element.9.s_ref, f32[8,32,512]{2,1,0:T(8,128)S(1)} %convert_element_type.23.sums_ref, bf16[2048,256]{1,0:T(8,128)(2,1)S(1)} %shard_map.28.unit_ref, bf16[2048,256]{1,0:T(8,128)(2,1)S(1)} %shard_map.29.more_ref), custom_call_target="tpu_custom_call" | custom-call | flops 402653184 | bytes 1572864 | tf_op jit(solution)/shard_map/pallas_call | solution.py:182
  73.0 0.1 convert_element_type.24
  73.2 18.4 %all_to_all.27 = f16[12,16,2048]{2,1,0:T(8,128)(2,1)S(1)} all-to-all(f16[12,16,2048]{2,1,0:T(8,128)(2,1)S(1)} %bitcast.3), channel_id=1, replica_groups=mesh['y'=8,'zh'=4,'zl'=3,'x'=4,'c'=2] {'zl','x'}, dimensions={0} | all-to-all | bytes 1572864 | tf_op jit(solution)/shard_map/all_to_all | solution.py:190
  91.5 0.1 convert_reduce_fusion
  91.7 15.7 %all_to_all.28 = f16[4,4,2048]{2,1,0:T(4,128)(2,1)S(1)} all-to-all(f16[4,4,2048]{2,1,0:T(4,128)(2,1)S(1)} %convert_element_type.27), channel_id=1, replica_groups=mesh['y'=8,'zh'=4,'zl'=3,'x'=4,'c'=2] {'zh'}, dimensions={0} | all-to-all | bytes 131072 | tf_op jit(solution)/shard_map/all_to_all | solution.py:192
  107.4 0.7 convert_reduce_fusion.1
  (6 shorter events, 0.1 us)
Async XLA Ops:
  0.0 32.8 %copy-start = (bf16[2048,256]{1,0:T(8,128)(2,1)S(1)}, bf16[2048,256]{1,0:T(8,128)(2,1)}, u32[]{:S(2)}) copy-start(bf16[2048,256]{1,0:T(8,128)(2,1)} %dir_ref.1) | copy-start | bytes 3145732
  26.9 19.1 %all-to-all-start.1 = ((bf16[12,16,2048]{2,1,0:T(8,128)(2,1)}), bf16[12,16,2048]{2,1,0:T(8,128)(2,1)S(1)}, u32[]{:S(2)}, u32[]{:S(2)}) async-start(bf16[12,16,2048]{2,1,0:T(8,128)(2,1)} %broadcast_in_dim.10), calls=%async_computation.1 | async-start | bytes 1572864 | tf_op jit(solution)/shard_map/near/all_to_all | solution.py:142
  32.8 4.5 %collective-permute-start = (bf16[2048,256]{1,0:T(8,128)(2,1)S(1)}, bf16[2048,256]{1,0:T(8,128)(2,1)S(1)}, u32[]{:S(2)}, u32[]{:S(2)}) collective-permute-start(bf16[2048,256]{1,0:T(8,128)(2,1)S(1)} %copy-done), channel_id=1, source_target_pairs={{0,1},{1,0},{2,3},{3,2},{4,5},{5,4},{6,7},{7,6},{8,9},{9,8},{10,11... | collective-permute-start | bytes 3145736 | tf_op jit(solution)/shard_map/columns/ppermute | solution.py:147
  48.4 3.1 %collective-permute-start.1 = (f32[32,512]{1,0:T(8,128)S(1)}, f32[32,512]{1,0:T(8,128)S(1)}, u32[]{:S(2)}, u32[]{:S(2)}) collective-permute-start(f32[32,512]{1,0:T(8,128)S(1)} %get-tuple-element.10), channel_id=1, source_target_pairs={{0,1},{1,0},{2,3},{3,2},{4,5},{5,4},{6,7},{7,6},{8,9},{9,8},{10,11... | collective-permute-start | bytes 196616 | tf_op jit(solution)/shard_map/ppermute | solution.py:147
